TPU v7x, 32 devices: a whole 2x2x4 slice. The times are simulated.
32 devices in a mesh: dp: 2 (over x), expert: 8 (over z, y), tensor: 2 (over core).
Axes of the slice: x: 2, y: 2, z: 4, core: 2. Of those that a mesh axis runs over, the one named last changes fastest.
Arguments:
- activations: bfloat16 [4096, 1536], P(('dp', 'expert', 'tensor')), may hold values from -6 to 6
- segments: int32 [16, 256], P(('dp', 'expert')), may hold values from 0 to 3, never falling along the last dimension, each value on 1 to 128 neighbouring positions
- routes: int32 [4096, 8], P(('dp', 'expert', 'tensor')), may hold values from 0 to 15, all different within a row; in each aligned block of 128 rows (0 to 127, 128 to 255, ...) at most 128 rows name the same one
- route_weights: float32 [4096, 8], P(('dp', 'expert', 'tensor')), may hold values from 0.03 to 0.3
- norm_attn_gain: float32 [1536], replicated, may hold values from 0.5 to 1.5
- norm_ffn_gain: float32 [1536], replicated, may hold values from 0.5 to 1.5
- query_weight: bfloat16 [1536, 1536], P(None, 'tensor'), may hold values from -0.15625 to 0.15625
- key_matrix: bfloat16 [1536, 512], P(None, 'tensor'), may hold values from -0.15625 to 0.15625
- value_matrix: bfloat16 [1536, 512], P(None, 'tensor'), may hold values from -0.15625 to 0.15625
- output_projection_weight: bfloat16 [1536, 1536], P('tensor'), may hold values from -0.625 to 0.625
- expert_gate: bfloat16 [16, 1536, 512], P('expert', None, 'tensor'), may hold values from -0.15625 to 0.15625
- expert_up: bfloat16 [16, 1536, 512], P('expert', None, 'tensor'), may hold values from -0.15625 to 0.15625
- expert_down: bfloat16 [16, 512, 1536], P('expert', 'tensor'), may hold values from -0.5 to 0.5
- grad_output: bfloat16 [4096, 1536], P(('dp', 'expert', 'tensor')), may hold values from -6 to 6
Outputs:
- block_out: bfloat16 [4096, 1536], P(('dp', 'expert', 'tensor'))
- grad_input: float32 [4096, 1536], P(('dp', 'expert', 'tensor'))
- grad_norm_attn: float32 [1536], replicated
- grad_norm_ffn: float32 [1536], replicated
- grad_query: float32 [1536, 1536], P(None, 'tensor')
- grad_key: float32 [1536, 512], P(None, 'tensor')
- grad_value: float32 [1536, 512], P(None, 'tensor')
- grad_mixer: float32 [1536, 1536], P('tensor')
- grad_expert_gate: float32 [16, 1536, 512], P('expert', None, 'tensor')
- grad_expert_up: float32 [16, 1536, 512], P('expert', None, 'tensor')
- grad_expert_down: float32 [16, 512, 1536], P('expert', 'tensor')
Inputs may be any that keep to these rules, and one draw needn't show every extreme that they name: `routes`: each row names 8 different experts; in the rows of one device (aligned blocks of 128 rows) no expert is named more than 128 times, and one is named exactly 128 times in some block. `segments`: each sequence's numbers never fall; 4 documents of 1 to 128 positions, one of exactly 128.
All inputs are finite; a program needn't handle non-finite values.
Results may differ from a plain program's by a relative error of at most 0.01.
Values may be sent and summed in bfloat16 or wider, within the bound.
No kernel may reach another device: no remote copies, remote signals or barrier semaphores. Data moves between devices by JAX's collectives and lax.ppermute only.
A program may use at most 320 MiB of HBM per device.

v0:
```python
import jax
import jax.numpy as jnp
from jax import lax
from jax.sharding import PartitionSpec as P

HEAD_DIM = 64
EPS = 1e-05
ATTN_SCALE = 0.015625
THETA = 10000.0
NEG_FILL = -1e30


def norm_forward(values, gain_vector):
    inv_scale = lax.rsqrt(jnp.mean(values * values, axis=-1, keepdims=True) + EPS)
    return (values * inv_scale * gain_vector, inv_scale)


def norm_backward(values, inv_scale, gain_vector, upstream):
    weighted = upstream * gain_vector
    inner = jnp.mean(weighted * values, axis=-1, keepdims=True)
    value_gradient = inv_scale * weighted - values * (inv_scale * inv_scale * inv_scale) * inner
    grad_gain = jnp.sum(upstream * values * inv_scale, axis=0)
    return (value_gradient, grad_gain)


def rope_tables(length, head_size):
    position = jnp.arange(length, dtype=jnp.float32)
    frequency = THETA ** (-jnp.arange(head_size // 2, dtype=jnp.float32) * 2.0 / head_size)
    angle_table = position[:, None] * frequency[None, :]
    return (jnp.cos(angle_table)[:, None, :], jnp.sin(angle_table)[:, None, :])


def apply_rotary(field_in, cosine_lookup, sine_lookup):
    half_size = field_in.shape[-1] // 2
    first_half = field_in[..., :half_size]
    second_half = field_in[..., half_size:]
    return jnp.concatenate(
        [
            first_half * cosine_lookup - second_half * sine_lookup,
            second_half * cosine_lookup + first_half * sine_lookup,
        ],
        axis=-1,
    )


def invert_rotary(field_in, cosine_lookup, sine_lookup):
    half_size = field_in.shape[-1] // 2
    first_half = field_in[..., :half_size]
    second_half = field_in[..., half_size:]
    return jnp.concatenate(
        [
            first_half * cosine_lookup + second_half * sine_lookup,
            second_half * cosine_lookup - first_half * sine_lookup,
        ],
        axis=-1,
    )


def mask_block(row_start, block_rows, seg_ids):
    length = seg_ids.shape[0]
    row_pos = row_start + jnp.arange(block_rows, dtype=jnp.int32)
    key_pos = jnp.arange(length, dtype=jnp.int32)
    return (key_pos[None, :] <= row_pos[:, None]) & (seg_ids[None, :] == seg_ids[:, None])


def block_scores(query_blk, key_heads, row_start, seg_ids):
    scores = (
        jnp.einsum("qhgd,khd->hgqk", query_blk, key_heads, preferred_element_type=jnp.float32)
        * ATTN_SCALE
    )
    allowed = mask_block(row_start, query_blk.shape[0], seg_ids)
    return jnp.where(allowed, scores, NEG_FILL)


def attend_block(query_blk, key_heads, value_head_rows, row_start, seg_ids):
    scores = block_scores(query_blk, key_heads, row_start, seg_ids)
    top_score = jnp.max(scores, axis=-1, keepdims=True)
    exp_total = jnp.sum(jnp.exp(scores - top_score), axis=-1, keepdims=True)
    log_total = top_score + jnp.log(exp_total)
    weights_soft = jnp.exp(scores - log_total).astype(jnp.bfloat16)
    mixed_heads = jnp.einsum(
        "hgqk,khd->qhgd", weights_soft, value_head_rows, preferred_element_type=jnp.float32
    )
    return (mixed_heads.astype(jnp.bfloat16), log_total[..., 0])


def attend_back(
    query_blk, key_heads, value_head_rows, log_total, grad_blk, mixed_blk, row_start, seg_ids
):
    scores = block_scores(query_blk, key_heads, row_start, seg_ids)
    weights_soft = jnp.exp(scores - log_total[..., None])
    row_delta = jnp.einsum(
        "qhgd,qhgd->hgq", grad_blk, mixed_blk, preferred_element_type=jnp.float32
    )
    grad_soft = jnp.einsum(
        "qhgd,khd->hgqk", grad_blk, value_head_rows, preferred_element_type=jnp.float32
    )
    grad_scores = (weights_soft * (grad_soft - row_delta[..., None]) * ATTN_SCALE).astype(
        jnp.bfloat16
    )
    grad_queries = jnp.einsum(
        "hgqk,khd->qhgd", grad_scores, key_heads, preferred_element_type=jnp.float32
    )
    key_gradient = jnp.einsum(
        "hgqk,qhgd->khd", grad_scores, query_blk, preferred_element_type=jnp.float32
    )
    value_gradient = jnp.einsum(
        "hgqk,qhgd->khd",
        weights_soft.astype(jnp.bfloat16),
        grad_blk,
        preferred_element_type=jnp.float32,
    )
    return (grad_queries, key_gradient, value_gradient)


def route_index(route_blk, expert_count, capacity):
    flat_routes = route_blk.reshape(-1)
    onehot = (flat_routes[:, None] == jnp.arange(expert_count, dtype=jnp.int32)[None, :]).astype(
        jnp.int32
    )
    earlier = jnp.cumsum(onehot, axis=0) - onehot
    slot_rank = jnp.sum(earlier * onehot, axis=1)
    return flat_routes * capacity + slot_rank


def body(
    activations,
    segments,
    routes,
    route_weights,
    norm_attn_gain,
    norm_ffn_gain,
    query_weight,
    key_matrix,
    value_matrix,
    output_projection_weight,
    expert_gate,
    expert_up,
    expert_down,
    grad_output,
):
    tensor_rank = lax.axis_index("tensor")
    tok_rows = activations.shape[0]
    model_width = activations.shape[1]
    experts_here = expert_gate.shape[0]
    expert_count = experts_here * lax.axis_size("expert")
    top_count = routes.shape[1]
    capacity = 2 * tok_rows * top_count // expert_count
    seg_ids = segments[0]
    length = seg_ids.shape[0]
    heads_q = query_weight.shape[1] // HEAD_DIM
    heads_kv = key_matrix.shape[1] // HEAD_DIM
    group_factor = heads_q // heads_kv
    block_rows = min(512, length)
    blocks = length // block_rows
    cosine_lookup, sine_lookup = rope_tables(length, HEAD_DIM)
    own_start = tensor_rank * tok_rows
    full_acts = lax.all_gather(activations, "tensor", axis=0, tiled=True)
    x_in = full_acts.astype(jnp.float32)
    normed_one, scale_one = norm_forward(x_in, norm_attn_gain)
    hidden_first = normed_one.astype(jnp.bfloat16)
    query_unrotated = jnp.dot(
        hidden_first, query_weight, preferred_element_type=jnp.float32
    ).reshape(length, heads_q, HEAD_DIM)
    query_head_rows = (
        apply_rotary(query_unrotated, cosine_lookup, sine_lookup)
        .astype(jnp.bfloat16)
        .reshape(length, heads_kv, group_factor, HEAD_DIM)
    )
    key_unrotated = jnp.dot(hidden_first, key_matrix, preferred_element_type=jnp.float32).reshape(
        length, heads_kv, HEAD_DIM
    )
    key_heads = apply_rotary(key_unrotated, cosine_lookup, sine_lookup).astype(jnp.bfloat16)
    value_head_rows = (
        jnp.dot(hidden_first, value_matrix, preferred_element_type=jnp.float32)
        .astype(jnp.bfloat16)
        .reshape(length, heads_kv, HEAD_DIM)
    )
    query_blocks = query_head_rows.reshape(blocks, block_rows, heads_kv, group_factor, HEAD_DIM)
    starts = jnp.arange(blocks, dtype=jnp.int32) * block_rows

    def forward_block(block_pair):
        return attend_block(block_pair[0], key_heads, value_head_rows, block_pair[1], seg_ids)

    mixed_heads, log_total = lax.map(forward_block, (query_blocks, starts))
    mixed_flat = mixed_heads.reshape(length, heads_q * HEAD_DIM)
    attn_part = jnp.dot(mixed_flat, output_projection_weight, preferred_element_type=jnp.float32)
    attn_out = lax.psum(attn_part, "tensor")
    residual = x_in + attn_out
    normed_two, scale_two = norm_forward(residual, norm_ffn_gain)
    h_two = normed_two.astype(jnp.bfloat16)
    h_own = lax.dynamic_slice_in_dim(h_two, own_start, tok_rows, 0)
    resid_own = lax.dynamic_slice_in_dim(residual, own_start, tok_rows, 0)
    slot_index = route_index(routes, expert_count, capacity)
    buffer = (
        jnp.zeros((expert_count * capacity, model_width), jnp.bfloat16)
        .at[slot_index]
        .set(jnp.repeat(h_own, top_count, axis=0))
        .reshape(expert_count, capacity, model_width)
    )
    received = lax.all_to_all(buffer, "expert", split_axis=0, concat_axis=1, tiled=True)
    gate_full, up_full, down_full = (expert_gate, expert_up, expert_down)
    rows_in = lax.all_gather(received, "tensor", axis=1, tiled=True)
    pre_gate = jnp.einsum("erd,edf->erf", rows_in, gate_full, preferred_element_type=jnp.float32)
    pre_up = jnp.einsum("erd,edf->erf", rows_in, up_full, preferred_element_type=jnp.float32)
    activated = (jax.nn.silu(pre_gate) * pre_up).astype(jnp.bfloat16)
    expert_part = jnp.einsum(
        "erf,efd->erd", activated, down_full, preferred_element_type=jnp.float32
    )
    expert_total = lax.psum_scatter(
        expert_part.astype(jnp.bfloat16), "tensor", scatter_dimension=1, tiled=True
    )
    returned = lax.all_to_all(expert_total, "expert", split_axis=1, concat_axis=0, tiled=True)
    picked = returned.reshape(-1, model_width)[slot_index].reshape(tok_rows, top_count, model_width)
    expert_mix = jnp.sum(route_weights[:, :, None] * picked.astype(jnp.float32), axis=1)
    block_out = (resid_own + expert_mix).astype(jnp.bfloat16)
    upstream_own = grad_output.astype(jnp.float32)
    grad_copies = (
        (route_weights[:, :, None] * upstream_own[:, None, :])
        .astype(jnp.bfloat16)
        .reshape(-1, model_width)
    )
    grad_buffer = (
        jnp.zeros((expert_count * capacity, model_width), jnp.bfloat16)
        .at[slot_index]
        .set(grad_copies)
        .reshape(expert_count, capacity, model_width)
    )
    grad_received = lax.all_to_all(grad_buffer, "expert", split_axis=0, concat_axis=1, tiled=True)
    grad_rows_in = lax.all_gather(grad_received, "tensor", axis=1, tiled=True)
    grad_down = jnp.einsum(
        "erf,erd->efd", activated, grad_rows_in, preferred_element_type=jnp.float32
    )
    grad_act = jnp.einsum(
        "erd,efd->erf", grad_rows_in, down_full, preferred_element_type=jnp.float32
    )
    gate_sigmoid = jax.nn.sigmoid(pre_gate)
    grad_pre_gate = (
        grad_act * pre_up * gate_sigmoid * (1.0 + pre_gate * (1.0 - gate_sigmoid))
    ).astype(jnp.bfloat16)
    grad_pre_up = (grad_act * pre_gate * gate_sigmoid).astype(jnp.bfloat16)
    grad_gate = jnp.einsum(
        "erd,erf->edf", rows_in, grad_pre_gate, preferred_element_type=jnp.float32
    )
    grad_up = jnp.einsum("erd,erf->edf", rows_in, grad_pre_up, preferred_element_type=jnp.float32)
    grad_in_part = jnp.einsum(
        "erf,edf->erd", grad_pre_gate, gate_full, preferred_element_type=jnp.float32
    ) + jnp.einsum("erf,edf->erd", grad_pre_up, up_full, preferred_element_type=jnp.float32)
    grad_in_rows = lax.psum_scatter(grad_in_part, "tensor", scatter_dimension=1, tiled=True)
    grad_back = lax.all_to_all(
        grad_in_rows.astype(jnp.bfloat16), "expert", split_axis=1, concat_axis=0, tiled=True
    )
    picked_grad = grad_back.reshape(-1, model_width)[slot_index].reshape(
        tok_rows, top_count, model_width
    )
    grad_h_own = jnp.sum(route_weights[:, :, None] * picked_grad.astype(jnp.float32), axis=1)
    upstream_full, grad_h_full = (
        lax.all_gather(upstream_own, "tensor", axis=0, tiled=True),
        lax.all_gather(grad_h_own, "tensor", axis=0, tiled=True),
    )
    grad_norm_part, grad_ffn_gain = norm_backward(residual, scale_two, norm_ffn_gain, grad_h_full)
    grad_resid = upstream_full + grad_norm_part
    residual_gradient_second = grad_resid.astype(jnp.bfloat16)
    grad_mix_w = jnp.einsum(
        "sa,sb->ab", mixed_flat, residual_gradient_second, preferred_element_type=jnp.float32
    )
    mixed_gradient = (
        jnp.einsum(
            "im,dm->id",
            residual_gradient_second,
            output_projection_weight,
            preferred_element_type=jnp.float32,
        )
        .astype(jnp.bfloat16)
        .reshape(blocks, block_rows, heads_kv, group_factor, HEAD_DIM)
    )

    def backward_block(block_pack):
        return attend_back(
            block_pack[0],
            key_heads,
            value_head_rows,
            block_pack[1],
            block_pack[2],
            block_pack[3],
            block_pack[4],
            seg_ids,
        )

    grad_queries, key_gradient, value_gradient = lax.map(
        backward_block, (query_blocks, log_total, mixed_gradient, mixed_heads, starts)
    )
    key_gradient = jnp.sum(key_gradient, axis=0)
    value_gradient = jnp.sum(value_gradient, axis=0)
    grad_q_rows = (
        invert_rotary(grad_queries.reshape(length, heads_q, HEAD_DIM), cosine_lookup, sine_lookup)
        .astype(jnp.bfloat16)
        .reshape(length, heads_q * HEAD_DIM)
    )
    grad_key_rows = (
        invert_rotary(key_gradient, cosine_lookup, sine_lookup)
        .astype(jnp.bfloat16)
        .reshape(length, heads_kv * HEAD_DIM)
    )
    grad_value_rows = value_gradient.astype(jnp.bfloat16).reshape(length, heads_kv * HEAD_DIM)
    grad_q_w = jnp.einsum(
        "sd,sa->da", hidden_first, grad_q_rows, preferred_element_type=jnp.float32
    )
    grad_k_w = jnp.einsum(
        "sd,sa->da", hidden_first, grad_key_rows, preferred_element_type=jnp.float32
    )
    grad_v_w = jnp.einsum(
        "sd,sa->da", hidden_first, grad_value_rows, preferred_element_type=jnp.float32
    )
    grad_h_part = (
        jnp.einsum("sa,da->sd", grad_q_rows, query_weight, preferred_element_type=jnp.float32)
        + jnp.einsum("sa,da->sd", grad_key_rows, key_matrix, preferred_element_type=jnp.float32)
        + jnp.einsum("sa,da->sd", grad_value_rows, value_matrix, preferred_element_type=jnp.float32)
    )
    grad_h_one = lax.psum(grad_h_part, "tensor")
    grad_x_part, grad_attn_gain = norm_backward(x_in, scale_one, norm_attn_gain, grad_h_one)
    grad_full = grad_resid + grad_x_part
    grad_input = lax.dynamic_slice_in_dim(grad_full, own_start, tok_rows, 0)
    dense_sums = lax.psum(
        (grad_attn_gain, grad_ffn_gain, grad_q_w, grad_k_w, grad_v_w, grad_mix_w), ("dp", "expert")
    )
    gate_half, up_half, down_half = (grad_gate, grad_up, grad_down)
    gate_sum, up_sum, down_sum = lax.psum((gate_half, up_half, down_half), "dp")
    return (
        block_out,
        grad_input,
        dense_sums[0],
        dense_sums[1],
        dense_sums[2],
        dense_sums[3],
        dense_sums[4],
        dense_sums[5],
        gate_sum,
        up_sum,
        down_sum,
    )


def solution(mesh):
    placed = (
        P(("dp", "expert", "tensor"), None),
        P(("dp", "expert"), None),
        P(("dp", "expert", "tensor"), None),
        P(("dp", "expert", "tensor"), None),
        P(),
        P(),
        P(None, "tensor"),
        P(None, "tensor"),
        P(None, "tensor"),
        P("tensor", None),
        P("expert", None, "tensor"),
        P("expert", None, "tensor"),
        P("expert", "tensor", None),
        P(("dp", "expert", "tensor"), None),
    )
    return jax.shard_map(
        body,
        mesh=mesh,
        in_specs=placed,
        out_specs=(
            P(("dp", "expert", "tensor"), None),
            P(("dp", "expert", "tensor"), None),
            P(),
            P(),
            P(None, "tensor"),
            P(None, "tensor"),
            P(None, "tensor"),
            P("tensor", None),
            P("expert", None, "tensor"),
            P("expert", None, "tensor"),
            P("expert", "tensor", None),
        ),
        check_vma=False,
    )
```

profile of v0, /device:TPU:0, one launch (start us, length us, event | category | flops | bytes accessed | tf_op | source)
XLA Modules:
  0.0 1433.3 jit_solution(16432259173664442176)
XLA Ops:
  9.0 4.5 reduce-window.6
  16.2 9.6 scatter_custom_fusion.1
  25.8 7.4 all-to-all-start.2
  33.3 3.2 all_gather.15
  37.7 1.7 fusion.56
  39.5 1.2 fusion.54
  46.1 1.9 fusion.59
  48.1 123.4 %all-to-all-done.2 = bf16[16,128,1536]{2,1,0:T(8,128)(2,1)} async-done(((bf16[16,128,1536]{2,1,0:T(8,128)(2,1)}), bf16[16,128,1536]{2,1,0:T(8,128)(2,1)}, u32[]{:S(2)}, u32[]{:S(2)}) %all-to-all-start.2) | async-done | bytes 6291488 | tf_op jit(solution)/shard_map/all_to_all | solution.py:229
  171.5 6.0 copy.77
  177.6 1.7 multiply_reduce_fusion.2
  180.6 9.9 scatter_custom_fusion
  190.5 142.7 %all_to_all.66 = bf16[16,128,1536]{2,1,0:T(8,128)(2,1)S(1)} all-to-all(bf16[16,128,1536]{2,1,0:T(8,128)(2,1)} %bitcast.164), channel_id=1, replica_groups=mesh['dp'=2,'expert'=8,'tensor'=2] {'expert'}, dimensions={0} | all-to-all | bytes 12582912 | tf_op jit(solution)/shard_map/all_to_all | solution.py:201
  333.2 3.3 copy.73
  336.6 11.0 fusion.61
  347.6 12.6 all-gather.5.cloned.1.call-done
  360.2 7.0 fusion.60
  367.2 9.4 multiply_convert_fusion.2
  376.6 1.3 copy-done.3
  378.0 6.4 convolution_convert_fusion
  384.6 19.7 %fusion.62 = f32[2,2048,1536]{2,1,0:T(8,128)} fusion(bf16[2,2048,256]{2,1,0:T(8,128)(2,1)} %get-tuple-element.84, bf16[2,1536,256]{2,1,0:T(8,128)(2,1)} %param.24), kind=kOutput, calls=%fused_computation.122 | convolution fusion | flops 3221225472 | bytes 28835840 | tf_op jit(solution)/shard_map/erf,edf->erd/dot_general | solution.py:246
  404.3 21.5 %convolution_add_fusion = f32[2,2048,1536]{2,1,0:T(8,128)} fusion(f32[2,2048,1536]{2,1,0:T(8,128)} %fusion.62, bf16[2,2048,256]{2,1,0:T(8,128)(2,1)} %get-tuple-element.85, bf16[2,1536,256]{2,1,0:T(8,128)(2,1)} %param.25), kind=kOutput, calls=%fused_computation.4 | convolution fusion | flops 3227516928 | bytes 54001664 | tf_op jit(solution)/shard_map/erf,edf->erd/dot_general | solution.py:248
  425.8 12.8 copy.74
  438.7 5.8 all-to-all-start.1
  444.5 18.1 %reduce-scatter.5.cloned.1.call-done = f32[2,1024,1536]{2,1,0:T(8,128)} async-done(((f32[2,2048,1536]{2,1,0:T(8,128)}), f32[2,1024,1536]{2,1,0:T(8,128)}) %reduce-scatter.5.cloned.1.call-update) | async-done | bytes 12582928 | tf_op jit(solution)/shard_map/reduce_scatter | solution.py:249
  462.6 8.0 convert_element_type.120
  470.6 12.7 copy.78
  483.4 99.8 %all-to-all-done.1 = bf16[2,1024,1536]{2,0,1:T(2,128)(2,1)} async-done(((bf16[2,1024,1536]{2,0,1:T(2,128)(2,1)}), bf16[2,1024,1536]{2,0,1:T(2,128)(2,1)}, u32[]{:S(2)}, u32[]{:S(2)}) %all-to-all-start.1) | async-done | bytes 6291488 | tf_op jit(solution)/shard_map/all_to_all | solution.py:213
  583.1 4.7 all-to-all-start.3
  588.4 6.7 copy.75
  595.1 10.9 gather_fusion
  606.0 119.7 %all-to-all-done.3 = bf16[2,1024,1536]{2,0,1:T(2,128)(2,1)} async-done(((bf16[2,1024,1536]{2,0,1:T(2,128)(2,1)}), bf16[2,1024,1536]{2,0,1:T(2,128)(2,1)}, u32[]{:S(2)}, u32[]{:S(2)}) %all-to-all-start.3) | async-done | bytes 6291488 | tf_op jit(solution)/shard_map/all_to_all | solution.py:250
  725.6 6.7 copy.79
  732.3 10.9 gather_fusion.1
  743.1 8.7 fusion
  752.9 12.1 fusion.64
  765.0 2.9 multiply_reduce_fusion
  767.9 6.2 all-gather.7.cloned.1.call-done
  774.1 2.8 subtract_add_fusion
  779.0 2.9 fusion.23
  782.1 1.1 fusion.7
  787.9 1.6 convolution_add_fusion.1
  789.8 11.8 fusion.65
  801.7 10.4 fusion.66
  813.2 2.6 fusion.48
  815.9 1.7 fusion.50
  817.5 3.1 fusion.52
  820.7 3.0 fusion.27
  823.8 1.4 convert_element_type.102
  826.7 2.9 fusion.21
  829.7 78.3 %all-reduce = (f32[1536]{0:T(1024)}, f32[1536]{0:T(1024)}) all-reduce(f32[1536]{0:T(1024)S(1)} %get-tuple-element.56, f32[1536]{0:T(1024)S(1)} %copy-done.51), channel_id=1, replica_groups=mesh['dp'=2,'expert'=8,'tensor'=2] {'dp','expert'}, use_global_device_ids=true, to_apply=%region_18.19 | all-reduce | flops 3072 | bytes 24576 | tf_op jit(solution)/shard_map/psum | solution.py:324
  908.0 2.7 dynamic-slice_add_fusion
  910.8 127.0 %all-reduce.14.cloned.1.call-done = (f32[2,1536,256]{2,1,0:T(8,128)}, f32[2,1536,256]{2,1,0:T(8,128)}, f32[2,256,1536]{2,1,0:T(8,128)}) async-done(((f32[2,1536,256]{2,1,0:T(8,128)}, f32[2,1536,256]{2,1,0:T(8,128)}, f32[2,256,1536]{2,1,0:T(8,128)}), (f32[2,1536,256]{2,1,0:T(8,128)}, f32[2,1536,256]{2,1,0:T(8,128)}, f32[2,256,1536]{2,1,0:T(8,128)})) %all-reduce.14.cloned.1.call-update) | async-done | bytes 9437200 | tf_op jit(solution)/shard_map/psum | solution.py:328
  1037.7 368.7 %all-reduce.12.cloned.1.call-done = (f32[1536,768]{1,0:T(8,128)}, f32[1536,256]{1,0:T(8,128)}, f32[1536,256]{1,0:T(8,128)}, f32[768,1536]{1,0:T(8,128)}) async-done(((f32[1536,768]{1,0:T(8,128)}, f32[1536,256]{1,0:T(8,128)}, f32[1536,256]{1,0:T(8,128)}, f32[768,1536]{1,0:T(8,128)}), (f32[1536,768]{1,0:T(8,128)}, f32[1536,256]{1,0:T(8,128)}, f32[1536,256]{1,0:T(8,128)}, ...) | async-done | bytes 12582928 | tf_op jit(solution)/shard_map/psum | solution.py:324
  1406.4 5.0 copy.119
  1411.4 1.1 copy.120
  1412.6 1.1 copy.121
  1413.7 1.2 copy-done.11
  1414.9 2.4 copy.122
  1417.3 1.2 copy-done.18
  1418.5 1.7 copy.123
  1420.2 1.4 copy-done.17
  1421.5 1.7 copy.124
  1423.2 1.4 copy-done.16
  1424.5 1.7 copy.125
  (189 shorter events, 24.1 us)
Async XLA Ops:
  7.2 38.9 %copy-start = (bf16[768,1536]{1,0:T(8,128)(2,1)S(1)}, bf16[768,1536]{1,0:T(8,128)(2,1)}, u32[]{:S(2)}) copy-start(bf16[768,1536]{1,0:T(8,128)(2,1)} %param.23) | copy-start | bytes 7077892
  15.2 10.6 copy-start.8
  25.8 11.7 copy-start.54
  25.8 11.8 copy-start.40
  25.8 145.6 %all-to-all-start.2 = ((bf16[16,128,1536]{2,1,0:T(8,128)(2,1)}), bf16[16,128,1536]{2,1,0:T(8,128)(2,1)}, u32[]{:S(2)}, u32[]{:S(2)}) async-start(bf16[16,128,1536]{2,1,0:T(8,128)(2,1)} %bitcast.162), calls=%async_computation.3 | async-start | bytes 12582912 | tf_op jit(solution)/shard_map/all_to_all | solution.py:229
  33.3 144.3 %all-reduce.8.cloned.1.call-start = ((), (), s32[]{:S(2)}) async-start(), calls=%async_computation.6 | async-start | bytes 3145728 | tf_op jit(solution)/shard_map/psum | solution.py:188
  33.3 6.1 copy-start.20
  36.5 141.1 %copy-start.1 = (bf16[256,1536]{1,0:T(8,128)(2,1)}, bf16[256,1536]{1,0:T(8,128)(2,1)S(1)}, u32[]{:S(2)}) copy-start(bf16[256,1536]{1,0:T(8,128)(2,1)S(1)} %all_gather.15) | copy-start | bytes 2359300
  37.3 5.5 copy-start.49
  37.5 3.1 copy-start.28
  37.5 3.1 copy-start.30
  37.7 6.8 copy-start.46
  39.5 1.4 copy-start.42
  39.5 1.4 copy-start.44
  40.8 1.3 copy-start.34
  42.1 2.3 copy-start.14
  42.2 1.7 copy-start.37
  43.9 1.5 copy-start.52
  48.0 288.6 %all-gather.9.cloned.1.call-start = ((), (), s32[]{:S(2)}) async-start(), calls=%async_computation.10 | async-start | bytes 18874368 | tf_op jit(solution)/shard_map/all_gather | solution.py:230
  177.5 2.9 copy-start.48
  177.5 182.6 %all-gather.5.cloned.1.call-start = ((), (), s32[]{:S(2)}) async-start(), calls=%async_computation.7 | async-start | bytes 18874368 | tf_op jit(solution)/shard_map/all_gather | solution.py:203
  179.3 1.1 copy-start.4
  336.5 89.3 %reduce-scatter.3.cloned.1.call-start = ((), (), s32[]{:S(2)}) async-start(), calls=%async_computation.8 | async-start | bytes 18874368 | tf_op jit(solution)/shard_map/reduce_scatter | solution.py:210
  360.2 7.0 copy-start.22
  360.2 7.0 copy-start.58
  367.2 10.8 copy-start.25
  376.6 1.3 copy-start.3
  384.3 78.2 %reduce-scatter.5.cloned.1.call-start = ((), (), s32[]{:S(2)}) async-start(), calls=%async_computation.11 | async-start | bytes 37748736 | tf_op jit(solution)/shard_map/reduce_scatter | solution.py:249
  438.7 144.5 %all-to-all-start.1 = ((bf16[2,1024,1536]{2,0,1:T(2,128)(2,1)}), bf16[2,1024,1536]{2,0,1:T(2,128)(2,1)}, u32[]{:S(2)}, u32[]{:S(2)}) async-start(bf16[2,1024,1536]{2,0,1:T(2,128)(2,1)} %copy.74), calls=%async_computation.2 | async-start | bytes 12582912 | tf_op jit(solution)/shard_map/all_to_all | solution.py:213
  583.1 142.5 %all-to-all-start.3 = ((bf16[2,1024,1536]{2,0,1:T(2,128)(2,1)}), bf16[2,1024,1536]{2,0,1:T(2,128)(2,1)}, u32[]{:S(2)}, u32[]{:S(2)}) async-start(bf16[2,1024,1536]{2,0,1:T(2,128)(2,1)} %copy.78), calls=%async_computation.5 | async-start | bytes 12582912 | tf_op jit(solution)/shard_map/all_to_all | solution.py:250
  587.9 177.1 %all-gather.11.cloned.1.call-start = ((), (), s32[]{:S(2)}) async-start(), calls=%async_computation.12 | async-start | bytes 2359296 | tf_op jit(solution)/shard_map/all_gather | solution.py:259
  751.9 22.2 %all-gather.7.cloned.1.call-start = ((), (), s32[]{:S(2)}) async-start(), calls=%async_computation.9 | async-start | bytes 2359296 | tf_op jit(solution)/shard_map/all_gather | solution.py:258
  752.6 74.0 %all-reduce.10.cloned.1.call-start = ((), (), s32[]{:S(2)}) async-start(), calls=%async_computation.13 | async-start | bytes 3145728 | tf_op jit(solution)/shard_map/psum | solution.py:320
  776.8 1.1 copy-start.6
  779.0 2.9 copy-start.10
  779.0 3.0 copy-start.15
  779.0 3.0 copy-start.47
  779.0 3.0 copy-start.57
  781.9 5.4 copy-start.39
  782.1 1.2 copy-start.43
  782.1 1.2 copy-start.45
  783.3 1.6 copy-start.29
  783.3 1.6 copy-start.31
  784.3 1.7 copy-start.21
  785.1 2.2 copy-start.12
  785.1 1.7 copy-start.36
  786.8 1.2 copy-start.38
  789.6 248.1 %all-reduce.14.cloned.1.call-start = ((), (), s32[]{:S(2)}) async-start(), calls=%async_computation.15 | async-start | bytes 18874368 | tf_op jit(solution)/shard_map/psum | solution.py:328
  812.1 1.1 copy-start.41
  812.1 1.1 copy-start.50
  812.1 594.3 %all-reduce.12.cloned.1.call-start = ((), (), s32[]{:S(2)}) async-start(), calls=%async_computation.14 | async-start | bytes 25165824 | tf_op jit(solution)/shard_map/psum | solution.py:324
  813.2 2.6 copy-start.27
  813.2 4.3 copy-start.13
  817.5 3.1 copy-start.7
  823.7 1.5 copy-start.55
  823.7 1.9 copy-start.5
  823.7 2.2 copy-start.19
  826.7 3.0 copy-start.51
  1406.4 5.0 copy-start.24
  1406.4 6.1 copy-start.23
  1411.4 3.5 copy-start.11
  1414.9 3.6 copy-start.18
  1418.5 3.0 copy-start.17
  1421.5 3.0 copy-start.16
  (8 other events, 7.1 us)
Sparse Core Ops, SparseCore 0:
  48.2 21.7 all-reduce.7
  177.6 23.4 all-gather.8
  336.6 23.4 all-gather.4
  384.4 22.6 reduce-scatter.2
  425.9 36.6 reduce-scatter.4
  752.0 8.8 all-gather.10
  763.0 10.9 all-gather.6
  789.7 21.5 all-reduce.9
  814.5 223.1 all-reduce.13
  1044.6 361.8 all-reduce.11
where the time goes:
time: 1440 us; the launch traced here: 1430 us
  waiting for transfers between devices  876 us (61%)
  blocking collectives  224 us (16%)
  matrix products  135 us (9%)
  local copies, waits for them, and re-layouts  112 us (8%)
  other arithmetic  50.5 us (4%)
  starting transfers between devices  19.3 us (1%)
  between operations  15.2 us (1%)
    psum x1, waiting for transfers between devices, body(): lax.psum((grad_attn_gain, grad_ffn_gain, grad_q_w, grad_k_w, grad_v_w, gr...  369 us
    all_to_all x1, blocking collectives, body(): lax.all_to_all(buffer, 'expert', split_axis=0, concat_axis=1, tiled=True)  143 us
    psum x1, waiting for transfers between devices, body(): gate_sum, up_sum, down_sum = lax.psum((gate_half, up_half, down_half), 'dp')  127 us
    all_to_all x1, waiting for transfers between devices, body(): lax.all_to_all(grad_buffer, 'expert', split_axis=0, concat_axis=1, tiled=...  123 us
    all_to_all x1, waiting for transfers between devices, body(): lax.all_to_all(grad_in_rows.astype(jnp.bfloat16), 'expert', split_axis=1,...  120 us
    all_to_all x1, waiting for transfers between devices, body(): lax.all_to_all(expert_total, 'expert', split_axis=1, concat_axis=0, tiled...  99.8 us
    psum x1, blocking collectives, body(): lax.psum((grad_attn_gain, grad_ffn_gain, grad_q_w, grad_k_w, grad_v_w, gr...  78.3 us
    unnamed x127, local copies, waits for them, and re-layouts  31.3 us
  transfers between devices with their start and end apart: 13, of which 8 were waited for; matrix products, arithmetic and copies ran while one was open for 13% of the time, Pallas kernels for 0%

commit v1 on v0

--- a/solution.py
+++ b/solution.py
@@ -321,8 +321,9 @@
     grad_x_part, grad_attn_gain = norm_backward(x_in, scale_one, norm_attn_gain, grad_h_one)
     grad_full = grad_resid + grad_x_part
     grad_input = lax.dynamic_slice_in_dim(grad_full, own_start, tok_rows, 0)
-    dense_sums = lax.psum(
-        (grad_attn_gain, grad_ffn_gain, grad_q_w, grad_k_w, grad_v_w, grad_mix_w), ("dp", "expert")
+    _reach_rings = lambda inner_x: lax.psum(lax.psum(inner_x, "expert"), "dp")
+    dense_sums = _reach_rings(
+        (grad_attn_gain, grad_ffn_gain, grad_q_w, grad_k_w, grad_v_w, grad_mix_w)
     )
     gate_half, up_half, down_half = (grad_gate, grad_up, grad_down)
     gate_sum, up_sum, down_sum = lax.psum((gate_half, up_half, down_half), "dp")

time: 1440 us -> 1760 us (1.22)
  waiting for transfers between devices: 876 us -> 1220 us
  blocking collectives: 224 us -> 191 us
    psum x2, waiting for transfers between devices: 496 us -> 813 us  [body(): _reach_rings = lambda inner_x: lax.psum(lax.psum(inner_x, 'expert'), 'dp')]
    psum x1 -> x2, blocking collectives: 78.3 us -> 46.3 us  [body(): _reach_rings = lambda inner_x: lax.psum(lax.psum(inner_x, 'expert'), 'dp')]
    psum x1, waiting for transfers between devices: 0.01 us -> 18.7 us  [body(): grad_h_one = lax.psum(grad_h_part, 'tensor')]
  transfers between devices with their start and end apart: 13 -> 13, of which waited for: 8 -> 10; matrix products, arithmetic and copies ran while one was open for 13% -> 11% of each run, Pallas kernels for 0% -> 0%
where the time goes in v1:
time: 1760 us; the launch traced here: 1750 us
  waiting for transfers between devices  1220 us (69%)
  blocking collectives  191 us (11%)
  matrix products  135 us (8%)
  local copies, waits for them, and re-layouts  112 us (6%)
  other arithmetic  54.2 us (3%)
  starting transfers between devices  19.3 us (1%)
    psum x2, waiting for transfers between devices, body(): _reach_rings = lambda inner_x: lax.psum(lax.psum(inner_x, 'expert'), 'dp')  813 us
    all_to_all x1, blocking collectives, body(): lax.all_to_all(buffer, 'expert', split_axis=0, concat_axis=1, tiled=True)  142 us
    all_to_all x1, waiting for transfers between devices, body(): lax.all_to_all(grad_buffer, 'expert', split_axis=0, concat_axis=1, tiled=...  124 us
    all_to_all x1, waiting for transfers between devices, body(): lax.all_to_all(grad_in_rows.astype(jnp.bfloat16), 'expert', split_axis=1,...  120 us
    all_to_all x1, waiting for transfers between devices, body(): lax.all_to_all(expert_total, 'expert', split_axis=1, concat_axis=0, tiled...  99.7 us
    psum x2, blocking collectives, body(): _reach_rings = lambda inner_x: lax.psum(lax.psum(inner_x, 'expert'), 'dp')  46.3 us
  transfers between devices with their start and end apart: 13, of which 10 were waited for; matrix products, arithmetic and copies ran while one was open for 11% of the time, Pallas kernels for 0%

profile of v1, /device:TPU:0, one launch (start us, length us, event | category | flops | bytes accessed | tf_op | source)
XLA Modules:
  0.0 1751.0 jit_solution(180023876507142427)
XLA Ops:
  10.1 4.5 reduce-window.6
  16.2 9.6 scatter_custom_fusion.1
  25.8 7.4 all-to-all-start.2
  33.3 3.0 all_gather.15
  38.2 1.7 fusion.56
  45.8 1.9 fusion.59
  47.9 123.6 %all-to-all-done.2 = bf16[16,128,1536]{2,1,0:T(8,128)(2,1)} async-done(((bf16[16,128,1536]{2,1,0:T(8,128)(2,1)}), bf16[16,128,1536]{2,1,0:T(8,128)(2,1)}, u32[]{:S(2)}, u32[]{:S(2)}) %all-to-all-start.2) | async-done | bytes 6291488 | tf_op jit(solution)/shard_map/all_to_all | solution.py:229
  171.4 6.0 copy.77
  177.5 1.7 multiply_reduce_fusion.2
  181.3 10.3 scatter_custom_fusion
  191.5 142.2 %all_to_all.66 = bf16[16,128,1536]{2,1,0:T(8,128)(2,1)S(1)} all-to-all(bf16[16,128,1536]{2,1,0:T(8,128)(2,1)} %bitcast.166), channel_id=1, replica_groups=mesh['dp'=2,'expert'=8,'tensor'=2] {'expert'}, dimensions={0} | all-to-all | bytes 12582912 | tf_op jit(solution)/shard_map/all_to_all | solution.py:201
  333.7 3.3 copy.73
  337.1 11.0 fusion.61
  348.1 12.5 all-gather.5.cloned.1.call-done
  360.6 7.0 fusion.60
  367.6 9.4 multiply_convert_fusion.2
  377.0 1.4 copy-done.1
  378.4 6.3 convolution_convert_fusion
  385.0 19.7 %fusion.62 = f32[2,2048,1536]{2,1,0:T(8,128)} fusion(bf16[2,2048,256]{2,1,0:T(8,128)(2,1)} %get-tuple-element.90, bf16[2,1536,256]{2,1,0:T(8,128)(2,1)} %param.24), kind=kOutput, calls=%fused_computation.122 | convolution fusion | flops 3221225472 | bytes 28835840 | tf_op jit(solution)/shard_map/erf,edf->erd/dot_general | solution.py:246
  404.7 21.5 %convolution_add_fusion = f32[2,2048,1536]{2,1,0:T(8,128)} fusion(f32[2,2048,1536]{2,1,0:T(8,128)} %fusion.62, bf16[2,2048,256]{2,1,0:T(8,128)(2,1)} %get-tuple-element.91, bf16[2,1536,256]{2,1,0:T(8,128)(2,1)} %param.25), kind=kOutput, calls=%fused_computation.4 | convolution fusion | flops 3227516928 | bytes 54001664 | tf_op jit(solution)/shard_map/erf,edf->erd/dot_general | solution.py:248
  426.3 12.8 copy.74
  439.1 5.8 all-to-all-start.1
  444.8 18.2 %reduce-scatter.5.cloned.1.call-done = f32[2,1024,1536]{2,1,0:T(8,128)} async-done(((f32[2,2048,1536]{2,1,0:T(8,128)}), f32[2,1024,1536]{2,1,0:T(8,128)}) %reduce-scatter.5.cloned.1.call-update) | async-done | bytes 12582928 | tf_op jit(solution)/shard_map/reduce_scatter | solution.py:249
  463.0 8.0 convert_element_type.120
  471.0 12.7 copy.78
  483.8 99.7 %all-to-all-done.1 = bf16[2,1024,1536]{2,0,1:T(2,128)(2,1)} async-done(((bf16[2,1024,1536]{2,0,1:T(2,128)(2,1)}), bf16[2,1024,1536]{2,0,1:T(2,128)(2,1)}, u32[]{:S(2)}, u32[]{:S(2)}) %all-to-all-start.1) | async-done | bytes 6291488 | tf_op jit(solution)/shard_map/all_to_all | solution.py:213
  583.5 4.7 all-to-all-start.3
  588.7 6.7 copy.75
  595.5 10.9 gather_fusion
  606.3 119.7 %all-to-all-done.3 = bf16[2,1024,1536]{2,0,1:T(2,128)(2,1)} async-done(((bf16[2,1024,1536]{2,0,1:T(2,128)(2,1)}), bf16[2,1024,1536]{2,0,1:T(2,128)(2,1)}, u32[]{:S(2)}, u32[]{:S(2)}) %all-to-all-start.3) | async-done | bytes 6291488 | tf_op jit(solution)/shard_map/all_to_all | solution.py:250
  726.0 6.7 copy.79
  732.7 10.9 gather_fusion.1
  743.5 8.7 fusion
  753.3 8.0 all-gather.11.cloned.1.call-done
  761.3 2.9 multiply_reduce_fusion
  764.7 9.8 all-gather.7.cloned.1.call-done
  774.5 2.8 subtract_add_fusion
  778.4 1.6 convolution_convert_fusion.2
  779.9 1.9 copy.80
  783.0 2.9 fusion.23
  788.7 3.0 fusion.27
  791.8 1.7 fusion.48
  793.6 1.7 fusion.50
  795.3 3.1 fusion.52
  798.5 10.5 fusion.66
  811.3 1.6 convolution_add_fusion.1
  813.2 11.9 fusion.64
  825.1 12.0 fusion.65
  837.1 363.3 %all-reduce.13.cloned.1.call-done = (f32[1536,768]{1,0:T(8,128)}, f32[1536,256]{1,0:T(8,128)}, f32[1536,256]{1,0:T(8,128)}, f32[768,1536]{1,0:T(8,128)}) async-done(((f32[1536,768]{1,0:T(8,128)}, f32[1536,256]{1,0:T(8,128)}, f32[1536,256]{1,0:T(8,128)}, f32[768,1536]{1,0:T(8,128)}), (f32[1536,768]{1,0:T(8,128)}, f32[1536,256]{1,0:T(8,128)}, f32[1536,256]{1,0:T(8,128)}, ...) | async-done | bytes 12582928 | tf_op jit(solution)/shard_map/psum | solution.py:324
  1200.5 1.3 convert_element_type.102
  1203.5 18.7 %all-reduce.11.cloned.1.call-done = f32[256,1536]{1,0:T(8,128)} async-done(((f32[256,1536]{1,0:T(8,128)}), f32[256,1536]{1,0:T(8,128)}) %all-reduce.11.cloned.1.call-update) | async-done | bytes 1572880 | tf_op jit(solution)/shard_map/psum | solution.py:320
  1222.1 2.9 fusion.21
  1225.1 37.3 %all-reduce = (f32[1536]{0:T(1024)S(1)}, f32[1536]{0:T(1024)S(1)}) all-reduce(f32[1536]{0:T(1024)S(1)} %get-tuple-element.56, f32[1536]{0:T(1024)S(1)} %copy-done.49), channel_id=1, replica_groups=mesh['dp'=2,'expert'=8,'tensor'=2] {'expert'}, use_global_device_ids=true, to_apply=%region_18.19 | all-reduce | flops 3072 | bytes 24576 | tf_op jit(solution)/shard_map/psum | solution.py:324
  1262.4 8.9 all-reduce.2
  1271.4 2.7 dynamic-slice_add_fusion
  1274.1 450.1 %all-reduce.15.cloned.1.call-done = (f32[1536,768]{1,0:T(8,128)}, f32[1536,256]{1,0:T(8,128)}, f32[1536,256]{1,0:T(8,128)}, f32[768,1536]{1,0:T(8,128)}, f32[2,1...) async-done(((f32[1536,768]{1,0:T(8,128)}, f32[1536,256]{1,0:T(8,128)}, f32[1536,256]{1,0:T(8,128)}, f32[768,1536]{1,0:T(8,128)}, ...) | async-done | bytes 22020112 | tf_op jit(solution)/shard_map/psum | solution.py:324
  1724.2 5.0 copy.123
  1732.7 2.4 copy.126
  1735.1 1.2 copy-done.12
  1736.3 1.7 copy.127
  1737.9 1.4 copy-done.11
  1739.3 1.7 copy.128
  1741.0 1.4 copy-done.10
  1742.3 1.7 copy.129
  (190 shorter events, 29.7 us)
Async XLA Ops:
  7.2 38.7 %copy-start = (bf16[768,1536]{1,0:T(8,128)(2,1)S(1)}, bf16[768,1536]{1,0:T(8,128)(2,1)}, u32[]{:S(2)}) copy-start(bf16[768,1536]{1,0:T(8,128)(2,1)} %param.23) | copy-start | bytes 7077892
  10.0 5.0 copy-start.34
  16.1 9.7 copy-start.6
  25.8 7.5 copy-start.37
  25.8 12.4 copy-start.38
  25.8 145.6 %all-to-all-start.2 = ((bf16[16,128,1536]{2,1,0:T(8,128)(2,1)}), bf16[16,128,1536]{2,1,0:T(8,128)(2,1)}, u32[]{:S(2)}, u32[]{:S(2)}) async-start(bf16[16,128,1536]{2,1,0:T(8,128)(2,1)} %bitcast.164), calls=%async_computation.3 | async-start | bytes 12582912 | tf_op jit(solution)/shard_map/all_to_all | solution.py:229
  33.2 144.3 %all-reduce.9.cloned.1.call-start = ((), (), s32[]{:S(2)}) async-start(), calls=%async_computation.6 | async-start | bytes 3145728 | tf_op jit(solution)/shard_map/psum | solution.py:188
  33.3 6.7 copy-start.14
  37.1 6.3 copy-start.47
  37.3 3.9 copy-start.23
  37.3 3.9 copy-start.25
  38.2 6.8 copy-start.44
  40.0 1.4 copy-start.40
  40.0 1.4 copy-start.42
  41.3 1.3 copy-start.29
  42.7 2.3 copy-start.8
  42.7 1.7 copy-start.32
  44.4 1.5 copy-start.50
  47.8 289.3 %all-gather.9.cloned.1.call-start = ((), (), s32[]{:S(2)}) async-start(), calls=%async_computation.10 | async-start | bytes 18874368 | tf_op jit(solution)/shard_map/all_gather | solution.py:230
  177.4 2.9 copy-start.46
  177.5 183.1 %all-gather.5.cloned.1.call-start = ((), (), s32[]{:S(2)}) async-start(), calls=%async_computation.7 | async-start | bytes 18874368 | tf_op jit(solution)/shard_map/all_gather | solution.py:203
  179.9 11.6 copy-start.52
  337.0 89.2 %reduce-scatter.3.cloned.1.call-start = ((), (), s32[]{:S(2)}) async-start(), calls=%async_computation.8 | async-start | bytes 18874368 | tf_op jit(solution)/shard_map/reduce_scatter | solution.py:210
  360.6 7.0 copy-start.16
  360.6 7.0 copy-start.58
  367.6 10.8 copy-start.20
  377.0 1.4 copy-start.1
  384.8 78.2 %reduce-scatter.5.cloned.1.call-start = ((), (), s32[]{:S(2)}) async-start(), calls=%async_computation.11 | async-start | bytes 37748736 | tf_op jit(solution)/shard_map/reduce_scatter | solution.py:249
  439.1 144.5 %all-to-all-start.1 = ((bf16[2,1024,1536]{2,0,1:T(2,128)(2,1)}), bf16[2,1024,1536]{2,0,1:T(2,128)(2,1)}, u32[]{:S(2)}, u32[]{:S(2)}) async-start(bf16[2,1024,1536]{2,0,1:T(2,128)(2,1)} %copy.74), calls=%async_computation.2 | async-start | bytes 12582912 | tf_op jit(solution)/shard_map/all_to_all | solution.py:213
  583.5 142.5 %all-to-all-start.3 = ((bf16[2,1024,1536]{2,0,1:T(2,128)(2,1)}), bf16[2,1024,1536]{2,0,1:T(2,128)(2,1)}, u32[]{:S(2)}, u32[]{:S(2)}) async-start(bf16[2,1024,1536]{2,0,1:T(2,128)(2,1)} %copy.78), calls=%async_computation.5 | async-start | bytes 12582912 | tf_op jit(solution)/shard_map/all_to_all | solution.py:250
  588.3 173.0 %all-gather.11.cloned.1.call-start = ((), (), s32[]{:S(2)}) async-start(), calls=%async_computation.12 | async-start | bytes 2359296 | tf_op jit(solution)/shard_map/all_gather | solution.py:259
  743.5 17.8 %copy-start.53 = (f32[256]{0:T(256)S(1)}, f32[256]{0:T(256)}, u32[]{:S(2)}) copy-start(f32[256]{0:T(256)} %copy-done.52) | copy-start | bytes 3076
  752.3 22.2 %copy-start.54 = (f32[256]{0:T(256)S(1)}, f32[256]{0:T(256)}, u32[]{:S(2)}) copy-start(f32[256]{0:T(256)} %get-tuple-element.102) | copy-start | bytes 3076
  752.3 22.2 %all-gather.7.cloned.1.call-start = ((), (), s32[]{:S(2)}) async-start(), calls=%async_computation.9 | async-start | bytes 2359296 | tf_op jit(solution)/shard_map/all_gather | solution.py:258
  753.0 447.4 %all-reduce.13.cloned.1.call-start = ((), (), s32[]{:S(2)}) async-start(), calls=%async_computation.14 | async-start | bytes 25165824 | tf_op jit(solution)/shard_map/psum | solution.py:324
  778.4 4.7 copy-start.51
  783.0 3.0 copy-start.9
  783.0 3.0 copy-start.19
  783.0 3.0 copy-start.45
  783.0 3.0 copy-start.57
  786.1 5.8 copy-start.35
  786.1 1.2 copy-start.30
  786.1 1.8 copy-start.41
  786.1 1.8 copy-start.43
  787.3 1.4 copy-start.5
  788.7 3.0 copy-start.24
  788.7 3.0 copy-start.26
  788.7 3.2 copy-start.39
  788.7 3.2 copy-start.48
  793.6 1.7 copy-start.21
  798.4 423.7 %all-reduce.11.cloned.1.call-start = ((), (), s32[]{:S(2)}) async-start(), calls=%async_computation.13 | async-start | bytes 3145728 | tf_op jit(solution)/shard_map/psum | solution.py:320
  798.5 10.5 copy-start.15
  809.0 1.2 copy-start.31
  812.9 911.3 %all-reduce.15.cloned.1.call-start = ((), (), s32[]{:S(2)}) async-start(), calls=%async_computation.15 | async-start | bytes 44040192 | tf_op jit(solution)/shard_map/psum | solution.py:324
  1200.4 1.4 copy-start.55
  1200.4 1.9 copy-start.3
  1200.5 2.2 copy-start.13
  1203.4 21.7 %copy-start.49 = (f32[1536]{0:T(1024)S(1)}, f32[1536]{0:T(1024)}, u32[]{:S(2)}) copy-start(f32[1536]{0:T(1024)} %get-tuple-element.54) | copy-start | bytes 18436
  1724.2 5.0 copy-start.18
  1724.2 6.1 copy-start.17
  1729.2 3.5 copy-start.7
  1732.7 3.6 copy-start.12
  1736.3 3.0 copy-start.11
  1739.3 3.0 copy-start.10
  (8 other events, 8.2 us)
Sparse Core Ops, SparseCore 0:
  47.9 21.7 all-reduce.8
  177.6 23.4 all-gather.8
  337.1 23.4 all-gather.4
  384.9 22.6 reduce-scatter.2
  426.4 36.6 reduce-scatter.4
  752.4 8.8 all-gather.10
  763.5 10.9 all-gather.6
  798.6 401.7 all-reduce.12
  1202.8 19.3 all-reduce.10
  1225.9 498.2 all-reduce.14
